TPU v7x, 512 devices: a whole 4x4x16 slice. The times are simulated.
512 devices in a mesh: seq: 4 (over y_lo, core), head: 8 (over x, y_hi), dp: 16 (over z).
Axes of the slice: x: 4, y: 4 (y_hi: 2, y_lo: 2; y = y_hi * 2 + y_lo), z: 16, core: 2. Of those that a mesh axis runs over, the one named last changes fastest.
Arguments:
- queries: bfloat16 [16, 2048, 4096], P('dp', 'seq', 'head'), may hold values from -2 to 2
- keys: bfloat16 [16, 2048, 4096], P('dp', 'seq', 'head'), may hold values from -2 to 2
- values: bfloat16 [16, 2048, 4096], P('dp', 'seq', 'head'), may hold values from -6 to 6
- out_proj: bfloat16 [4096, 1024], P('head', 'dp'), may hold values from -0.09375 to 0.09375
- depth_proj: bfloat16 [1024, 1024], P(None, ('head', 'dp')), may hold values from -0.1875 to 0.1875
- code_table: bfloat16 [2, 1024, 1024], P(None, ('head', 'dp')), may hold values from -6 to 6
- code_ids: int32 [16, 2048, 2], P('dp', ('seq', 'head')), may hold values from 0 to 1023
- depth_cotangent: bfloat16 [16, 2048, 2, 1024], P('dp', ('seq', 'head')), may hold values from -6 to 6
Outputs:
- grad_queries: bfloat16 [16, 2048, 4096], P('dp', 'seq', 'head')
- grad_keys: bfloat16 [16, 2048, 4096], P('dp', 'seq', 'head')
- grad_values: bfloat16 [16, 2048, 4096], P('dp', 'seq', 'head')
- grad_out_proj: float32 [4096, 1024], P('head', 'dp')
All inputs are finite; a program needn't handle non-finite values.
Results may differ from a plain program's by a relative error of at most 0.024.
Values may be sent and summed in bfloat16 or wider, within the bound.
A program may use at most 64 MiB of HBM per device.

v0:
```python
import jax
import jax.numpy as jnp
from jax import lax
from jax.sharding import PartitionSpec as P

DH = 128


def from_behind(block, axis, distance):
    devices = range(lax.axis_size(axis))
    route = [(i - distance, i) for i in devices if i - distance in devices]
    return lax.ppermute(block, axis, route)


def causal_mask(size):
    places = jnp.arange(size, dtype=jnp.int32)
    return (places[:, None] >= places[None, :]).astype(jnp.float32)


def depth_forward(carried, code_tab, proj_mat, code_rows):
    vocab_idx = jnp.arange(code_tab.shape[1], dtype=jnp.int32)
    level_outs = []
    for level_idx in range(code_tab.shape[0]):
        onehot = (code_rows[:, level_idx][:, None] == vocab_idx[None, :]).astype(jnp.bfloat16)
        embedded = jnp.dot(onehot, code_tab[level_idx], preferred_element_type=jnp.float32)
        summed = carried + embedded
        normed = (
            summed * lax.rsqrt(jnp.mean(summed * summed, axis=-1, keepdims=True) + 1e-05)
        ).astype(jnp.bfloat16)
        projected = jnp.dot(normed, proj_mat, preferred_element_type=jnp.float32)
        level_outs.append(projected)
        carried = summed + jax.nn.silu(projected)
    return jnp.stack(level_outs, axis=1)


def on_device(queries, keys, values, out_proj, depth_proj, code_table, code_ids, depth_cotangent):
    group_len = queries.shape[1]
    width_dev = queries.shape[2]
    heads_here = width_dev // DH
    att_scale = float(group_len * lax.axis_size("seq")) ** (-0.5)
    query_rows = queries[0].reshape(group_len, heads_here, DH)
    key_rows = keys[0].reshape(group_len, heads_here, DH)
    value_rows = values[0].reshape(group_len, heads_here, DH)
    causal = causal_mask(group_len)
    state_zero = jnp.zeros((heads_here, DH, DH), jnp.float32)
    state_local = jnp.einsum(
        "thd,the->hde", key_rows, value_rows, preferred_element_type=jnp.float32
    )
    state_acc = state_zero
    moving = state_local
    for hop_idx in range(lax.axis_size("seq") - 1):
        moving = from_behind(moving.astype(jnp.bfloat16), "seq", 1).astype(moving.dtype)
        state_acc = state_acc + moving
    state_in = state_acc.astype(jnp.bfloat16)
    scores = (
        jnp.einsum("thd,shd->hts", query_rows, key_rows, preferred_element_type=jnp.float32)
        * causal
    ).astype(jnp.bfloat16)
    attended = (
        att_scale
        * (
            jnp.einsum("hts,she->the", scores, value_rows, preferred_element_type=jnp.float32)
            + jnp.einsum("thd,hde->the", query_rows, state_in, preferred_element_type=jnp.float32)
        )
    ).astype(jnp.bfloat16)
    attended_flat = attended.reshape(group_len, width_dev)
    proj_full = lax.all_gather(out_proj, "dp", axis=1, tiled=True)
    mixed = lax.psum_scatter(
        jnp.dot(attended_flat, proj_full, preferred_element_type=jnp.float32).astype(jnp.bfloat16),
        "head",
        scatter_dimension=0,
        tiled=True,
    ).astype(jnp.float32)
    proj_mat, code_tab = (
        lax.all_gather(depth_proj, ("head", "dp"), axis=1, tiled=True),
        lax.all_gather(code_table, ("head", "dp"), axis=1, tiled=True),
    )
    code_rows = code_ids[0]
    cotangent = depth_cotangent[0].astype(jnp.float32)
    _, pullback = jax.vjp(
        lambda inputs: depth_forward(inputs, code_tab, proj_mat, code_rows), mixed
    )
    grad_mixed = pullback(cotangent)[0].astype(jnp.bfloat16)
    grad_block = lax.all_gather(grad_mixed, "head", axis=0, tiled=True)
    grad_att = lax.dot_general(
        grad_block, proj_full, (((1,), (1,)), ((), ())), preferred_element_type=jnp.float32
    )
    grad_rows = grad_att.astype(jnp.bfloat16).reshape(group_len, heads_here, DH)
    weight_term = lax.dot_general(
        attended_flat, grad_block, (((0,), (0,)), ((), ())), preferred_element_type=jnp.float32
    )
    weight_part = lax.psum_scatter(
        weight_term.astype(jnp.bfloat16), "dp", scatter_dimension=1, tiled=True
    )
    grad_out_proj = lax.psum(weight_part, "seq").astype(jnp.float32)
    back_local = jnp.einsum(
        "thd,the->hde", query_rows, grad_rows, preferred_element_type=jnp.float32
    )
    back_acc = state_zero
    moving_back = back_local
    for hop_idx in range(lax.axis_size("seq") - 1):
        moving_back = from_behind(moving_back.astype(jnp.bfloat16), "seq", -1).astype(
            moving_back.dtype
        )
        back_acc = back_acc + moving_back
    back_state = back_acc.astype(jnp.bfloat16)
    grad_scores = (
        jnp.einsum("the,she->hts", grad_rows, value_rows, preferred_element_type=jnp.float32)
        * causal
    ).astype(jnp.bfloat16)
    grad_query = att_scale * (
        jnp.einsum("hts,shd->thd", grad_scores, key_rows, preferred_element_type=jnp.float32)
        + jnp.einsum("the,hde->thd", grad_rows, state_in, preferred_element_type=jnp.float32)
    )
    grad_key = att_scale * (
        jnp.einsum("hts,thd->shd", grad_scores, query_rows, preferred_element_type=jnp.float32)
        + jnp.einsum("she,hde->shd", value_rows, back_state, preferred_element_type=jnp.float32)
    )
    grad_value = att_scale * (
        jnp.einsum("hts,the->she", scores, grad_rows, preferred_element_type=jnp.float32)
        + jnp.einsum("shd,hde->she", key_rows, back_state, preferred_element_type=jnp.float32)
    )
    out_shape = (1, group_len, width_dev)
    return (
        grad_query.reshape(out_shape).astype(jnp.bfloat16),
        grad_key.reshape(out_shape).astype(jnp.bfloat16),
        grad_value.reshape(out_shape).astype(jnp.bfloat16),
        grad_out_proj,
    )


def solution(mesh):
    in_specs = (
        P("dp", "seq", "head"),
        P("dp", "seq", "head"),
        P("dp", "seq", "head"),
        P("head", "dp"),
        P(None, ("head", "dp")),
        P(None, ("head", "dp"), None),
        P("dp", ("seq", "head"), None),
        P("dp", ("seq", "head"), None, None),
    )
    out_specs = (
        P("dp", "seq", "head"),
        P("dp", "seq", "head"),
        P("dp", "seq", "head"),
        P("head", "dp"),
    )
    return jax.shard_map(
        on_device, mesh=mesh, in_specs=in_specs, out_specs=out_specs, check_vma=False
    )
```

profile of v0, /device:TPU:1, one launch (start us, length us, event | category | flops | bytes accessed | tf_op | source)
XLA Modules:
  0.0 812.8 jit_solution(11603275540361019960)
XLA Ops:
  8.7 1.2 reshape_squeeze.10
  10.7 4.6 collective-permute-start
  16.4 3.3 collective-permute-done
  19.7 1.9 collective-permute-start.1
  21.6 2.0 multiply_convert_fusion.1
  23.6 4.2 collective-permute-start.2
  28.7 1.1 collective-permute-done.2
  29.8 1.2 fusion.9
  31.0 44.8 %all-gather.7.cloned.1.call-done = bf16[512,1024]{0,1:T(8,128)(2,1)} async-done(((bf16[512,64]{0,1:T(8,128)(2,1)}), bf16[512,1024]{0,1:T(8,128)(2,1)}) %all-gather.7.cloned.1.call-update) | async-done | bytes 1048592 | tf_op jit(solution)/shard_map/all_gather | solution.py:67
  75.7 3.2 convolution_convert_fusion.1
  79.6 1.7 copy.57
  81.3 210.8 %all-gather.5.cloned.1.call-done = bf16[1024,1024]{0,1:T(8,128)(2,1)} async-done(((bf16[1024,8]{0,1:T(8,128)(2,1)}), bf16[1024,1024]{0,1:T(8,128)(2,1)}) %all-gather.5.cloned.1.call-update) | async-done | bytes 2097168 | tf_op jit(solution)/shard_map/all_gather | solution.py:75
  292.2 2.1 fusion.16
  294.3 92.4 %reduce-scatter.3.cloned.1.call-done = bf16[64,1024]{1,0:T(8,128)(2,1)} async-done(((bf16[512,1024]{1,0:T(8,128)(2,1)}), bf16[64,1024]{1,0:T(8,128)(2,1)}) %reduce-scatter.3.cloned.1.call-update) | async-done | bytes 131088 | tf_op jit(solution)/shard_map/reduce_scatter | solution.py:68
  386.7 218.7 %all-gather.9.cloned.1.call-done = bf16[2,1024,1024]{2,1,0:T(8,128)(2,1)} async-done(((bf16[2,8,1024]{2,1,0:T(8,128)(2,1)}), bf16[2,1024,1024]{2,1,0:T(8,128)(2,1)}) %all-gather.9.cloned.1.call-update) | async-done | bytes 4194320 | tf_op jit(solution)/shard_map/all_gather | solution.py:76
  605.5 2.4 multiply_reduce_fusion.3
  608.6 2.3 multiply_reduce_fusion.2
  612.6 64.7 %all-gather.11.cloned.1.call-done = bf16[512,1024]{1,0:T(8,128)(2,1)} async-done(((bf16[64,1024]{1,0:T(8,128)(2,1)}), bf16[512,1024]{1,0:T(8,128)(2,1)}) %all-gather.11.cloned.1.call-update) | async-done | bytes 1048592 | tf_op jit(solution)/shard_map/all_gather | solution.py:84
  677.3 3.1 convolution_convert_fusion
  680.5 2.4 convolution_convert_fusion.2
  683.2 4.3 collective-permute-start.3
  687.5 1.4 fusion.45
  690.3 1.9 collective-permute-start.4
  693.1 3.6 collective-permute-done.4
  696.7 1.9 collective-permute-start.5
  699.7 2.1 copy.29
  701.8 1.5 collective-permute-done.5
  703.3 2.1 fusion.12
  705.4 36.8 %reduce-scatter.5.cloned.1.call-done = bf16[512,64]{0,1:T(8,128)(2,1)} async-done(((bf16[512,1024]{0,1:T(8,128)(2,1)}), bf16[512,64]{0,1:T(8,128)(2,1)}) %reduce-scatter.5.cloned.1.call-update) | async-done | bytes 65552 | tf_op jit(solution)/shard_map/reduce_scatter | solution.py:92
  742.3 1.3 fusion.11
  745.6 58.9 %all-reduce.2.cloned.1.call-done = bf16[512,64]{0,1:T(8,128)(2,1)} async-done(((bf16[512,64]{0,1:T(8,128)(2,1)}), bf16[512,64]{0,1:T(8,128)(2,1)}) %all-reduce.2.cloned.1.call-update) | async-done | bytes 65552 | tf_op jit(solution)/shard_map/psum | solution.py:95
  804.5 1.5 convert_element_type.168
  (82 shorter events, 12.8 us)
Async XLA Ops:
  7.2 3.1 copy-start.20
  7.2 68.6 %all-gather.7.cloned.1.call-start = ((), (), s32[]{:S(2)}) async-start(), calls=%async_computation.3 | async-start | bytes 1114112 | tf_op jit(solution)/shard_map/all_gather | solution.py:67
  7.9 284.3 %all-gather.5.cloned.1.call-start = ((), (), s32[]{:S(2)}) async-start(), calls=%async_computation.2 | async-start | bytes 2113536 | tf_op jit(solution)/shard_map/all_gather | solution.py:75
  8.7 6.7 copy-start.21
  8.7 378.1 %reduce-scatter.3.cloned.1.call-start = ((), (), s32[]{:S(2)}) async-start(), calls=%async_computation.4 | async-start | bytes 1179648 | tf_op jit(solution)/shard_map/reduce_scatter | solution.py:68
  9.9 5.4 copy-start.7
  10.3 5.0 copy-start.10
  10.4 9.3 %copy-start.1 = (bf16[512,4,128]{2,1,0:T(4,128)(2,1)}, bf16[512,4,128]{2,1,0:T(4,128)(2,1)S(1)}, u32[]{:S(2)}) copy-start(bf16[512,4,128]{2,1,0:T(4,128)(2,1)S(1)} %reshape_squeeze.11) | copy-start | bytes 1572868
  10.7 9.0 %collective-permute-start = (bf16[4,128,128]{2,1,0:T(8,128)(2,1)S(1)}, bf16[4,128,128]{2,1,0:T(8,128)(2,1)S(1)}, u32[]{:S(2)}, u32[]{:S(2)}) collective-permute-start(bf16[4,128,128]{2,1,0:T(8,128)(2,1)S(1)} %convolution_convert_fusion.5), channel_id=1, source_target_pairs={{0,128},{128,256},{256,384},{1,129},{129,257},{257,385},{2,130},{1... | collective-permute-start | bytes 393224 | tf_op jit(solution)/shard_map/ppermute | solution.py:12
  19.7 3.9 collective-permute-start.1
  21.6 6.3 copy-start.2
  23.6 6.2 copy-start.5
  23.6 7.4 copy-start.14
  23.6 6.2 collective-permute-start.2
  29.8 49.2 %copy-start.16 = (bf16[4,128,128]{2,1,0:T(8,128)(2,1)}, bf16[4,128,128]{2,1,0:T(8,128)(2,1)S(1)}, u32[]{:S(2)}) copy-start(bf16[4,128,128]{2,1,0:T(8,128)(2,1)S(1)} %collective-permute-done.2) | copy-start | bytes 393220
  75.7 5.6 copy-start.22
  79.0 526.5 %all-gather.9.cloned.1.call-start = ((), (), s32[]{:S(2)}) async-start(), calls=%async_computation.5 | async-start | bytes 4227072 | tf_op jit(solution)/shard_map/all_gather | solution.py:76
  79.6 597.7 %all-gather.11.cloned.1.call-start = ((), (), s32[]{:S(2)}) async-start(), calls=%async_computation.6 | async-start | bytes 1179648 | tf_op jit(solution)/shard_map/all_gather | solution.py:84
  612.6 129.7 %reduce-scatter.5.cloned.1.call-start = ((), (), s32[]{:S(2)}) async-start(), calls=%async_computation.7 | async-start | bytes 1114112 | tf_op jit(solution)/shard_map/reduce_scatter | solution.py:92
  680.4 124.0 %all-reduce.2.cloned.1.call-start = ((), (), s32[]{:S(2)}) async-start(), calls=%async_computation.8 | async-start | bytes 131072 | tf_op jit(solution)/shard_map/psum | solution.py:95
  683.2 5.7 copy-start.3
  683.2 7.1 collective-permute-start.3
  690.2 8.4 %copy-start.15 = (bf16[4,128,128]{2,1,0:T(8,128)(2,1)S(1)}, bf16[4,128,128]{2,1,0:T(8,128)(2,1)}, u32[]{:S(2)}) copy-start(bf16[4,128,128]{2,1,0:T(8,128)(2,1)} %copy-done.14) | copy-start | bytes 393220
  690.2 8.4 %copy-start.17 = (bf16[4,128,128]{2,1,0:T(8,128)(2,1)S(1)}, bf16[4,128,128]{2,1,0:T(8,128)(2,1)}, u32[]{:S(2)}) copy-start(bf16[4,128,128]{2,1,0:T(8,128)(2,1)} %copy-done.16) | copy-start | bytes 393220
  690.3 9.4 %copy-start.18 = (bf16[4,128,128]{1,2,0:T(8,128)(2,1)}, bf16[4,128,128]{1,2,0:T(8,128)(2,1)S(1)}, u32[]{:S(2)}) copy-start(bf16[4,128,128]{1,2,0:T(8,128)(2,1)S(1)} %collective-permute-done.3) | copy-start | bytes 393220
  690.3 6.4 collective-permute-start.4
  693.1 10.2 %copy-start.8 = (bf16[512,4,128]{2,1,0:T(4,128)(2,1)S(1)}, bf16[512,4,128]{2,1,0:T(4,128)(2,1)}, u32[]{:S(2)}) copy-start(bf16[512,4,128]{2,1,0:T(4,128)(2,1)} %copy-done.7) | copy-start | bytes 1572868
  693.1 10.2 %copy-start.9 = (f32[4,128,512]{2,1,0:T(8,128)S(1)}, f32[4,128,512]{2,1,0:T(8,128)}, u32[]{:S(2)}) copy-start(f32[4,128,512]{2,1,0:T(8,128)} %fusion.45) | copy-start | bytes 3145732
  696.7 6.6 collective-permute-start.5
  699.7 42.5 %copy-start.4 = (bf16[512,4,128]{2,1,0:T(4,128)(2,1)S(1)}, bf16[512,4,128]{2,1,0:T(4,128)(2,1)}, u32[]{:S(2)}) copy-start(bf16[512,4,128]{2,1,0:T(4,128)(2,1)} %copy-done.1) | copy-start | bytes 1572868
  699.7 42.5 %copy-start.19 = (bf16[4,128,128]{1,2,0:T(8,128)(2,1)S(1)}, bf16[4,128,128]{1,2,0:T(8,128)(2,1)}, u32[]{:S(2)}) copy-start(bf16[4,128,128]{1,2,0:T(8,128)(2,1)} %copy-done.18) | copy-start | bytes 393220
  705.4 38.2 %copy-start.12 = (bf16[4,128,512]{2,1,0:T(8,128)(2,1)S(1)}, bf16[4,128,512]{2,1,0:T(8,128)(2,1)}, u32[]{:S(2)}) copy-start(bf16[4,128,512]{2,1,0:T(8,128)(2,1)} %fusion.12) | copy-start | bytes 1572868
  (4 other events, 9.7 us)
Sparse Core Ops, SparseCore 0:
  10.1 65.6 all-gather.6
  80.1 212.0 all-gather.4
  296.7 89.9 reduce-scatter.2
  391.0 214.4 all-gather.8
  612.7 64.5 all-gather.10
  680.6 61.6 reduce-scatter.4
  745.1 59.3 all-reduce.1
where the time goes:
time: 813 us
  waiting for transfers between devices  739 us (91%)
  matrix products  29.6 us (4%)
  starting transfers between devices  19.1 us (2%)
  between operations  14.6 us (2%)
  local copies, waits for them, and re-layouts  8.51 us (1%)
    all_gather x1, waiting for transfers between devices, on_device(): lax.all_gather(code_table, ('head', 'dp'), axis=1, tiled=True)  219 us
    all_gather x1, waiting for transfers between devices, on_device(): lax.all_gather(depth_proj, ('head', 'dp'), axis=1, tiled=True)  211 us
    reduce_scatter x1, waiting for transfers between devices, on_device(): lax.psum_scatter(jnp.dot(attended_flat, proj_full, preferred_element_type...  92.4 us
    all_gather x1, waiting for transfers between devices, on_device(): grad_block = lax.all_gather(grad_mixed, 'head', axis=0, tiled=True)  64.7 us
    psum x1, waiting for transfers between devices, on_device(): grad_out_proj = lax.psum(weight_part, 'seq').astype(jnp.float32)  58.9 us
    all_gather x1, waiting for transfers between devices, on_device(): proj_full = lax.all_gather(out_proj, 'dp', axis=1, tiled=True)  44.8 us
    reduce_scatter x1, waiting for transfers between devices, on_device(): lax.psum_scatter(weight_term.astype(jnp.bfloat16), 'dp', scatter_dimensio...  36.8 us
    ppermute x6, starting transfers between devices, from_behind(): return lax.ppermute(block, axis, route)  18.9 us
  transfers between devices with their start and end apart: 13, of which 12 were waited for; matrix products, arithmetic and copies ran while one was open for 4% of the time, Pallas kernels for 0%

commit v1 on v0

--- a/solution.py
+++ b/solution.py
@@ -92,7 +92,7 @@
     weight_part = lax.psum_scatter(
         weight_term.astype(jnp.bfloat16), "dp", scatter_dimension=1, tiled=True
     )
-    grad_out_proj = lax.psum(weight_part, "seq").astype(jnp.float32)
+    grad_out_proj = jnp.sum(lax.all_gather(weight_part, "seq"), axis=0).astype(jnp.float32)
     back_local = jnp.einsum(
         "thd,the->hde", query_rows, grad_rows, preferred_element_type=jnp.float32
     )

time: 813 us -> 772 us (0.950)
  waiting for transfers between devices: 739 us -> 679 us
  blocking collectives: 0 us -> 16.8 us
    psum x1 -> x0, waiting for transfers between devices: 58.9 us -> none  [on_device(): grad_out_proj = lax.psum(weight_part, 'seq').astype(jnp.float32)]
    all_gather x0 -> x1, blocking collectives: none -> 16.8 us  [on_device(): lax.all_gather(weight_part, 'seq')]
  transfers between devices with their start and end apart: 13 -> 12, of which waited for: 12 -> 10; matrix products, arithmetic and copies ran while one was open for 4% -> 4% of each run, Pallas kernels for 0% -> 0%
where the time goes in v1:
time: 772 us
  waiting for transfers between devices  679 us (88%)
  matrix products  30.1 us (4%)
  starting transfers between devices  19.1 us (2%)
  blocking collectives  16.8 us (2%)
  between operations  14.6 us (2%)
  local copies, waits for them, and re-layouts  10 us (1%)
    all_gather x1, waiting for transfers between devices, on_device(): lax.all_gather(code_table, ('head', 'dp'), axis=1, tiled=True)  219 us
    all_gather x1, waiting for transfers between devices, on_device(): lax.all_gather(depth_proj, ('head', 'dp'), axis=1, tiled=True)  211 us
    reduce_scatter x1, waiting for transfers between devices, on_device(): lax.psum_scatter(jnp.dot(attended_flat, proj_full, preferred_element_type...  92.4 us
    all_gather x1, waiting for transfers between devices, on_device(): grad_block = lax.all_gather(grad_mixed, 'head', axis=0, tiled=True)  64.7 us
    all_gather x1, waiting for transfers between devices, on_device(): proj_full = lax.all_gather(out_proj, 'dp', axis=1, tiled=True)  44.8 us
    reduce_scatter x1, waiting for transfers between devices, on_device(): lax.psum_scatter(weight_term.astype(jnp.bfloat16), 'dp', scatter_dimensio...  36.3 us
    ppermute x6, starting transfers between devices, from_behind(): return lax.ppermute(block, axis, route)  18.9 us
    all_gather x1, blocking collectives, on_device(): lax.all_gather(weight_part, 'seq')  16.8 us
  transfers between devices with their start and end apart: 12, of which 10 were waited for; matrix products, arithmetic and copies ran while one was open for 4% of the time, Pallas kernels for 0%

profile of v1, /device:TPU:1, one launch (start us, length us, event | category | flops | bytes accessed | tf_op | source)
XLA Modules:
  0.0 771.9 jit_solution(11836519828945985882)
XLA Ops:
  8.7 1.2 reshape_squeeze.10
  10.7 4.6 collective-permute-start
  16.4 3.3 collective-permute-done
  19.7 1.9 collective-permute-start.1
  21.6 2.0 multiply_convert_fusion.1
  23.6 4.2 collective-permute-start.2
  28.7 1.1 collective-permute-done.2
  29.8 1.2 fusion.9
  31.0 44.8 %all-gather.8.cloned.1.call-done = bf16[512,1024]{0,1:T(8,128)(2,1)} async-done(((bf16[512,64]{0,1:T(8,128)(2,1)}), bf16[512,1024]{0,1:T(8,128)(2,1)}) %all-gather.8.cloned.1.call-update) | async-done | bytes 1048592 | tf_op jit(solution)/shard_map/all_gather | solution.py:67
  75.7 3.2 convolution_convert_fusion.1
  79.6 1.7 copy.57
  81.4 210.8 %all-gather.6.cloned.1.call-done = bf16[1024,1024]{0,1:T(8,128)(2,1)} async-done(((bf16[1024,8]{0,1:T(8,128)(2,1)}), bf16[1024,1024]{0,1:T(8,128)(2,1)}) %all-gather.6.cloned.1.call-update) | async-done | bytes 2097168 | tf_op jit(solution)/shard_map/all_gather | solution.py:75
  292.2 2.1 fusion.16
  294.3 92.4 %reduce-scatter.3.cloned.1.call-done = bf16[64,1024]{1,0:T(8,128)(2,1)} async-done(((bf16[512,1024]{1,0:T(8,128)(2,1)}), bf16[64,1024]{1,0:T(8,128)(2,1)}) %reduce-scatter.3.cloned.1.call-update) | async-done | bytes 131088 | tf_op jit(solution)/shard_map/reduce_scatter | solution.py:68
  386.7 218.7 %all-gather.10.cloned.1.call-done = bf16[2,1024,1024]{2,1,0:T(8,128)(2,1)} async-done(((bf16[2,8,1024]{2,1,0:T(8,128)(2,1)}), bf16[2,1024,1024]{2,1,0:T(8,128)(2,1)}) %all-gather.10.cloned.1.call-update) | async-done | bytes 4194320 | tf_op jit(solution)/shard_map/all_gather | solution.py:76
  605.5 2.4 multiply_reduce_fusion.3
  608.6 2.3 multiply_reduce_fusion.2
  612.6 64.7 %all-gather.12.cloned.1.call-done = bf16[512,1024]{1,0:T(8,128)(2,1)} async-done(((bf16[64,1024]{1,0:T(8,128)(2,1)}), bf16[512,1024]{1,0:T(8,128)(2,1)}) %all-gather.12.cloned.1.call-update) | async-done | bytes 1048592 | tf_op jit(solution)/shard_map/all_gather | solution.py:84
  677.3 2.4 convolution_convert_fusion.2
  680.7 4.2 collective-permute-start.3
  684.9 1.7 convolution_convert_fusion
  686.7 2.5 fusion.45
  690.8 2.1 collective-permute-start.4
  693.7 3.8 collective-permute-done.4
  697.5 1.9 collective-permute-start.5
  700.6 2.1 copy.29
  702.7 1.5 collective-permute-done.5
  704.1 2.1 fusion.12
  706.3 2.0 copy.31
  708.3 1.4 fusion.11
  710.7 36.3 %reduce-scatter.5.cloned.1.call-done = bf16[512,64]{0,1:T(8,128)(2,1)} async-done(((bf16[512,1024]{0,1:T(8,128)(2,1)}), bf16[512,64]{0,1:T(8,128)(2,1)}) %reduce-scatter.5.cloned.1.call-update) | async-done | bytes 65552 | tf_op jit(solution)/shard_map/reduce_scatter | solution.py:92
  747.0 16.8 %all-gather = bf16[2048,64]{0,1:T(8,128)(2,1)S(1)} all-gather(bf16[512,64]{0,1:T(8,128)(2,1)} %reduce-scatter.5.cloned.1.call-done), channel_id=2, replica_groups=mesh['seq'=4,'head'=8,'dp'=16] {'seq'}, dimensions={0}, use_global_device_ids=true | all-gather | bytes 327680 | tf_op jit(solution)/shard_map/all_gather | solution.py:95
  (86 shorter events, 13.7 us)
Async XLA Ops:
  7.2 3.1 copy-start.21
  7.2 68.6 %all-gather.8.cloned.1.call-start = ((), (), s32[]{:S(2)}) async-start(), calls=%async_computation.3 | async-start | bytes 1114112 | tf_op jit(solution)/shard_map/all_gather | solution.py:67
  7.9 284.3 %all-gather.6.cloned.1.call-start = ((), (), s32[]{:S(2)}) async-start(), calls=%async_computation.2 | async-start | bytes 2113536 | tf_op jit(solution)/shard_map/all_gather | solution.py:75
  8.7 6.7 copy-start.22
  8.7 378.1 %reduce-scatter.3.cloned.1.call-start = ((), (), s32[]{:S(2)}) async-start(), calls=%async_computation.4 | async-start | bytes 1179648 | tf_op jit(solution)/shard_map/reduce_scatter | solution.py:68
  9.9 5.4 copy-start.8
  10.3 5.0 copy-start.13
  10.4 9.3 %copy-start.1 = (bf16[512,4,128]{2,1,0:T(4,128)(2,1)}, bf16[512,4,128]{2,1,0:T(4,128)(2,1)S(1)}, u32[]{:S(2)}) copy-start(bf16[512,4,128]{2,1,0:T(4,128)(2,1)S(1)} %reshape_squeeze.11) | copy-start | bytes 1572868
  10.7 9.0 %collective-permute-start = (bf16[4,128,128]{2,1,0:T(8,128)(2,1)S(1)}, bf16[4,128,128]{2,1,0:T(8,128)(2,1)S(1)}, u32[]{:S(2)}, u32[]{:S(2)}) collective-permute-start(bf16[4,128,128]{2,1,0:T(8,128)(2,1)S(1)} %convolution_convert_fusion.5), channel_id=1, source_target_pairs={{0,128},{128,256},{256,384},{1,129},{129,257},{257,385},{2,130},{1... | collective-permute-start | bytes 393224 | tf_op jit(solution)/shard_map/ppermute | solution.py:12
  19.7 3.9 collective-permute-start.1
  21.6 6.3 copy-start.2
  23.6 6.2 copy-start.5
  23.6 7.4 copy-start.17
  23.6 6.2 collective-permute-start.2
  29.8 49.2 %copy-start.19 = (bf16[4,128,128]{2,1,0:T(8,128)(2,1)}, bf16[4,128,128]{2,1,0:T(8,128)(2,1)S(1)}, u32[]{:S(2)}) copy-start(bf16[4,128,128]{2,1,0:T(8,128)(2,1)S(1)} %collective-permute-done.2) | copy-start | bytes 393220
  75.7 5.6 copy-start.23
  79.0 526.5 %all-gather.10.cloned.1.call-start = ((), (), s32[]{:S(2)}) async-start(), calls=%async_computation.5 | async-start | bytes 4227072 | tf_op jit(solution)/shard_map/all_gather | solution.py:76
  79.6 597.7 %all-gather.12.cloned.1.call-start = ((), (), s32[]{:S(2)}) async-start(), calls=%async_computation.6 | async-start | bytes 1179648 | tf_op jit(solution)/shard_map/all_gather | solution.py:84
  612.6 134.5 %reduce-scatter.5.cloned.1.call-start = ((), (), s32[]{:S(2)}) async-start(), calls=%async_computation.7 | async-start | bytes 1114112 | tf_op jit(solution)/shard_map/reduce_scatter | solution.py:92
  677.3 7.6 copy-start.16
  677.3 7.6 copy-start.24
  680.7 10.1 %collective-permute-start.3 = (bf16[4,128,128]{1,2,0:T(8,128)(2,1)}, bf16[4,128,128]{1,2,0:T(8,128)(2,1)}, u32[]{:S(2)}, u32[]{:S(2)}) collective-permute-start(bf16[4,128,128]{1,2,0:T(8,128)(2,1)} %fusion.17), channel_id=1, source_target_pairs={{128,0},{256,128},{384,256},{129,1},{257,129},{385,257},{130,2},{2... | collective-permute-start | bytes 393224 | tf_op jit(solution)/shard_map/ppermute | solution.py:12
  686.7 2.6 copy-start.3
  686.7 2.6 copy-start.11
  690.3 2.6 copy-start.14
  690.8 8.7 %copy-start.18 = (bf16[4,128,128]{2,1,0:T(8,128)(2,1)S(1)}, bf16[4,128,128]{2,1,0:T(8,128)(2,1)}, u32[]{:S(2)}) copy-start(bf16[4,128,128]{2,1,0:T(8,128)(2,1)} %copy-done.17) | copy-start | bytes 393220
  690.8 8.7 %copy-start.20 = (bf16[4,128,128]{2,1,0:T(8,128)(2,1)S(1)}, bf16[4,128,128]{2,1,0:T(8,128)(2,1)}, u32[]{:S(2)}) copy-start(bf16[4,128,128]{2,1,0:T(8,128)(2,1)} %copy-done.19) | copy-start | bytes 393220
  690.8 6.7 collective-permute-start.4
  693.7 10.4 %copy-start.9 = (bf16[512,4,128]{2,1,0:T(4,128)(2,1)S(1)}, bf16[512,4,128]{2,1,0:T(4,128)(2,1)}, u32[]{:S(2)}) copy-start(bf16[512,4,128]{2,1,0:T(4,128)(2,1)} %copy-done.8) | copy-start | bytes 1572868
  693.7 10.4 %copy-start.12 = (f32[4,128,512]{2,1,0:T(8,128)S(1)}, f32[4,128,512]{2,1,0:T(8,128)}, u32[]{:S(2)}) copy-start(f32[4,128,512]{2,1,0:T(8,128)} %fusion.45) | copy-start | bytes 3145732
  697.5 6.6 collective-permute-start.5
  700.6 7.8 %copy-start.4 = (bf16[512,4,128]{2,1,0:T(4,128)(2,1)S(1)}, bf16[512,4,128]{2,1,0:T(4,128)(2,1)}, u32[]{:S(2)}) copy-start(bf16[512,4,128]{2,1,0:T(4,128)(2,1)} %copy-done.1) | copy-start | bytes 1572868
  (5 other events, 9.2 us)
Sparse Core Ops, SparseCore 0:
  10.1 65.6 all-gather.7
  80.1 212.0 all-gather.5
  296.7 89.9 reduce-scatter.2
  391.0 214.4 all-gather.9
  612.7 64.5 all-gather.11
  686.8 60.2 reduce-scatter.4
